TPU v7x, 32 devices: a whole 2x2x4 slice. The times are simulated.
32 devices in a mesh: shard: 16 (over z, x, core), replica: 2 (over y).
Axes of the slice: x: 2, y: 2, z: 4, core: 2. Of those that a mesh axis runs over, the one named last changes fastest.
Arguments:
- x_in: bfloat16 [2, 8192, 768], P('replica', 'shard'), may hold values from -6 to 6
- seq_units: int32 [2, 16], P('replica'), may hold values from 1 to 64, 512 in all within a row
- deal: int32 [2, 16], P('replica'), may hold values from 0 to 15, each once within a row
- gain_attn: float32 [768], replicated, may hold values from 0.1 to 1.9
- w_query: bfloat16 [768, 768], P('shard'), may hold values from -0.4375 to 0.4375
- w_key: bfloat16 [768, 768], P('shard'), may hold values from -0.21875 to 0.21875
- w_value: bfloat16 [768, 768], P('shard'), may hold values from -0.21875 to 0.21875
- w_out: bfloat16 [768, 768], P('shard'), may hold values from -0.875 to 0.875
- gain_ffn: float32 [768], replicated, may hold values from 0.1 to 1.9
- w_gate: bfloat16 [768, 2048], P('shard'), may hold values from -0.21875 to 0.21875
- w_up: bfloat16 [768, 2048], P('shard'), may hold values from -0.21875 to 0.21875
- w_down: bfloat16 [2048, 768], P('shard'), may hold values from -0.125 to 0.125
- d_out: bfloat16 [2, 16, 1024, 768], P('replica', 'shard'), may hold values from -6 to 6
Outputs:
- layer_out: bfloat16 [2, 16, 1024, 768], P('replica', 'shard')
- grad_x: bfloat16 [2, 8192, 768], P('replica', 'shard')
- grad_gain_attn: float32 [768], P('shard')
- grad_gain_ffn: float32 [768], P('shard')
- grad_w_query: float32 [768, 768], P('shard')
- grad_w_key: float32 [768, 768], P('shard')
- grad_w_value: float32 [768, 768], P('shard')
- grad_w_out: float32 [768, 768], P('shard')
- grad_w_gate: float32 [768, 2048], P('shard')
- grad_w_up: float32 [768, 2048], P('shard')
- grad_w_down: float32 [2048, 768], P('shard')
Inputs may be any that keep to these rules, and one draw needn't show every extreme that they name: `seq_units`: each group's 16 entries sum to 512. `deal`: each group's row names every sequence 0 to 15 once.
All inputs are finite; a program needn't handle non-finite values.
Results may differ from a plain program's by a relative error of at most 0.023.
Values may be sent and summed in bfloat16 or wider, within the bound.
No kernel may reach another device: no remote copies, remote signals or barrier semaphores. Data moves between devices by JAX's collectives and lax.ppermute only.
A program may use at most 320 MiB of HBM per device.

v0:
```python
import jax
import jax.numpy as jnp
from jax import lax
from jax.sharding import PartitionSpec as P

H = 12
HD = 64
norm_eps = 1e-06
neg_big = -1e30


def rms_scale(tok_rows, gain_vec):
    inverse = lax.rsqrt(jnp.mean(tok_rows * tok_rows, axis=-1, keepdims=True) + norm_eps)
    return tok_rows * inverse * gain_vec


def gelu_mix(gate_vals, up_vals):
    return jax.nn.gelu(gate_vals, approximate=True) * up_vals


def lookup(table, wanted):
    table_slots = jnp.arange(table.shape[0], dtype=jnp.int32)
    return jnp.sum(jnp.where(wanted[:, None] == table_slots[None, :], table[None, :], 0), axis=1)


def left_dot(lhs_mat, rhs_mat):
    return lax.dot_general(
        lhs_mat, rhs_mat, (((0,), (0,)), ((), ())), preferred_element_type=jnp.float32
    )


def right_dot(lhs_mat, rhs_mat):
    return lax.dot_general(
        lhs_mat, rhs_mat, (((1,), (1,)), ((), ())), preferred_element_type=jnp.float32
    )


def plain_dot(lhs_mat, rhs_mat):
    return jnp.dot(lhs_mat, rhs_mat, preferred_element_type=jnp.float32)


def attend_forward(queries, keys_all, values_all, live_keys):
    total_rows = queries.shape[0]
    row_block = min(512, total_rows)
    factor = HD ** (-0.5)
    key_heads = keys_all.reshape(total_rows, H, HD)
    value_heads = values_all.reshape(total_rows, H, HD)
    mixed_list = []
    stat_list = []
    for row_begin in range(0, total_rows, row_block):
        query_heads = queries[row_begin : row_begin + row_block].reshape(row_block, H, HD)
        scores = (
            jnp.einsum("qhd,khd->hqk", query_heads, key_heads, preferred_element_type=jnp.float32)
            * factor
        )
        scores = jnp.where(live_keys[None, None, :], scores, neg_big)
        row_max = jnp.max(scores, axis=-1, keepdims=True)
        exp_vals = jnp.exp(scores - row_max)
        row_total = jnp.sum(exp_vals, axis=-1, keepdims=True)
        prob_vals = (exp_vals / row_total).astype(jnp.bfloat16)
        mixed_rows = jnp.einsum(
            "hqk,khd->qhd", prob_vals, value_heads, preferred_element_type=jnp.float32
        )
        mixed_list.append(mixed_rows.reshape(row_block, H * HD))
        stat_list.append(row_max + jnp.log(row_total))
    return (jnp.concatenate(mixed_list, axis=0), jnp.concatenate(stat_list, axis=1))


def attend_backward(queries, keys_all, values_all, live_keys, log_totals, grad_mixed):
    total_rows = queries.shape[0]
    row_block = min(512, total_rows)
    factor = HD ** (-0.5)
    key_heads = keys_all.reshape(total_rows, H, HD)
    value_heads = values_all.reshape(total_rows, H, HD)
    grad_keys = jnp.zeros((total_rows, H, HD), jnp.float32)
    grad_values = jnp.zeros((total_rows, H, HD), jnp.float32)
    query_list = []
    for row_begin in range(0, total_rows, row_block):
        query_heads = queries[row_begin : row_begin + row_block].reshape(row_block, H, HD)
        grad_heads = grad_mixed[row_begin : row_begin + row_block].reshape(row_block, H, HD)
        scores = (
            jnp.einsum("qhd,khd->hqk", query_heads, key_heads, preferred_element_type=jnp.float32)
            * factor
        )
        scores = jnp.where(live_keys[None, None, :], scores, neg_big)
        prob_vals = jnp.exp(scores - log_totals[:, row_begin : row_begin + row_block])
        grad_probs = jnp.einsum(
            "qhd,khd->hqk", grad_heads, value_heads, preferred_element_type=jnp.float32
        )
        row_dot = jnp.sum(prob_vals * grad_probs, axis=-1, keepdims=True)
        grad_scores = (prob_vals * (grad_probs - row_dot)).astype(jnp.bfloat16)
        grad_query = (
            jnp.einsum("hqk,khd->qhd", grad_scores, key_heads, preferred_element_type=jnp.float32)
            * factor
        )
        query_list.append(grad_query.reshape(row_block, H * HD))
        grad_keys = (
            grad_keys
            + jnp.einsum(
                "hqk,qhd->khd", grad_scores, query_heads, preferred_element_type=jnp.float32
            )
            * factor
        )
        grad_values = grad_values + jnp.einsum(
            "hqk,qhd->khd",
            prob_vals.astype(jnp.bfloat16),
            grad_heads,
            preferred_element_type=jnp.float32,
        )
    return (
        jnp.concatenate(query_list, axis=0),
        grad_keys.reshape(total_rows, H * HD),
        grad_values.reshape(total_rows, H * HD),
    )


def shards(
    x_in,
    seq_units,
    deal,
    gain_attn,
    w_query,
    w_key,
    w_value,
    w_out,
    gain_ffn,
    w_gate,
    w_up,
    w_down,
    d_out,
):
    shard_count = lax.axis_size("shard")
    my_index = lax.axis_index("shard")
    width = x_in.shape[2]
    span = d_out.shape[2]
    unit_max = span // shard_count
    units_row = seq_units[0]
    order_row = deal[0]
    offsets = jnp.cumsum(units_row) - units_row
    inner_idx = jnp.arange(unit_max, dtype=jnp.int32)
    dest_idx = jnp.arange(shard_count, dtype=jnp.int32)
    counts = lookup(units_row, order_row)
    starts = lookup(offsets, order_row)
    row_index = starts[:, None] + jnp.minimum(inner_idx[None, :], counts[:, None] - 1)
    sent_live = inner_idx[None, :] < counts[:, None]
    local_rows = x_in[0]
    outgoing = jnp.where(
        sent_live[:, :, None], local_rows[row_index], jnp.zeros((), local_rows.dtype)
    )
    arrived = lax.all_to_all(outgoing, "shard", split_axis=0, concat_axis=0, tiled=True)
    own_count = jnp.sum(jnp.where(dest_idx == my_index, counts, 0))
    live_rows = jnp.broadcast_to(inner_idx[None, :] < own_count, (shard_count, unit_max)).reshape(
        span
    )
    wq_full, wk_full, wv_full, wo_full = (
        lax.all_gather(w_query, "shard", axis=0, tiled=True),
        lax.all_gather(w_key, "shard", axis=0, tiled=True),
        lax.all_gather(w_value, "shard", axis=0, tiled=True),
        lax.all_gather(w_out, "shard", axis=0, tiled=True),
    )
    tok_float = arrived.reshape(span, width).astype(jnp.float32)
    normed_one_f, norm_one_back = jax.vjp(rms_scale, tok_float, gain_attn)
    normed_one = normed_one_f.astype(jnp.bfloat16)
    queries = plain_dot(normed_one, wq_full).astype(jnp.bfloat16)
    keys_all = plain_dot(normed_one, wk_full).astype(jnp.bfloat16)
    values_all = plain_dot(normed_one, wv_full).astype(jnp.bfloat16)
    mixed_f, log_totals = attend_forward(queries, keys_all, values_all, live_rows)
    mixed_rows = mixed_f.astype(jnp.bfloat16)
    hidden_res = tok_float + plain_dot(mixed_rows, wo_full)
    wg_full, wu_full, wd_full = (
        lax.all_gather(w_gate, "shard", axis=0, tiled=True),
        lax.all_gather(w_up, "shard", axis=0, tiled=True),
        lax.all_gather(w_down, "shard", axis=0, tiled=True),
    )
    normed_two_f, norm_two_back = jax.vjp(rms_scale, hidden_res, gain_ffn)
    normed_two = normed_two_f.astype(jnp.bfloat16)
    gate_vals = plain_dot(normed_two, wg_full)
    up_vals = plain_dot(normed_two, wu_full)
    act_f, mix_back = jax.vjp(gelu_mix, gate_vals, up_vals)
    act_vals = act_f.astype(jnp.bfloat16)
    result = jnp.where(live_rows[:, None], hidden_res + plain_dot(act_vals, wd_full), 0.0)
    layer_out = result.astype(jnp.bfloat16).reshape(1, 1, span, width)
    wg_back, wu_back, wd_back = (
        lax.all_gather(w_gate, "shard", axis=0, tiled=True),
        lax.all_gather(w_up, "shard", axis=0, tiled=True),
        lax.all_gather(w_down, "shard", axis=0, tiled=True),
    )
    grad_y = jnp.where(live_rows[:, None], d_out[0, 0].astype(jnp.float32), 0.0)
    grad_ffn_b = grad_y.astype(jnp.bfloat16)
    grad_down = left_dot(act_vals, grad_ffn_b)
    grad_act = right_dot(grad_ffn_b, wd_back)
    grad_gate_f, grad_up_f = mix_back(grad_act)
    grad_gate_b = grad_gate_f.astype(jnp.bfloat16)
    grad_up_b = grad_up_f.astype(jnp.bfloat16)
    grad_wg = left_dot(normed_two, grad_gate_b)
    grad_wu = left_dot(normed_two, grad_up_b)
    grad_n2 = right_dot(grad_gate_b, wg_back) + right_dot(grad_up_b, wu_back)
    grad_h_norm, grad_gain_two = norm_two_back(grad_n2)
    ffn_share = (
        lax.psum_scatter(
            grad_wg.astype(jnp.bfloat16), "shard", scatter_dimension=0, tiled=True
        ).astype(jnp.float32),
        lax.psum_scatter(
            grad_wu.astype(jnp.bfloat16), "shard", scatter_dimension=0, tiled=True
        ).astype(jnp.float32),
        lax.psum_scatter(
            grad_down.astype(jnp.bfloat16), "shard", scatter_dimension=0, tiled=True
        ).astype(jnp.float32),
        lax.psum_scatter(
            grad_gain_two.astype(jnp.bfloat16), "shard", scatter_dimension=0, tiled=True
        ).astype(jnp.float32),
    )
    grad_hidden = grad_y + grad_h_norm
    wq_back, wk_back, wv_back, wo_back = (
        lax.all_gather(w_query, "shard", axis=0, tiled=True),
        lax.all_gather(w_key, "shard", axis=0, tiled=True),
        lax.all_gather(w_value, "shard", axis=0, tiled=True),
        lax.all_gather(w_out, "shard", axis=0, tiled=True),
    )
    grad_attn_b = grad_hidden.astype(jnp.bfloat16)
    grad_wo = left_dot(mixed_rows, grad_attn_b)
    grad_mixed = right_dot(grad_attn_b, wo_back).astype(jnp.bfloat16)
    grad_q_f, grad_k_f, grad_v_f = attend_backward(
        queries, keys_all, values_all, live_rows, log_totals, grad_mixed
    )
    grad_q_b = grad_q_f.astype(jnp.bfloat16)
    grad_k_b = grad_k_f.astype(jnp.bfloat16)
    grad_v_b = grad_v_f.astype(jnp.bfloat16)
    grad_wq = left_dot(normed_one, grad_q_b)
    grad_wk = left_dot(normed_one, grad_k_b)
    grad_wv = left_dot(normed_one, grad_v_b)
    grad_n1 = (
        right_dot(grad_q_b, wq_back) + right_dot(grad_k_b, wk_back) + right_dot(grad_v_b, wv_back)
    )
    grad_x_norm, grad_gain_one = norm_one_back(grad_n1)
    grad_tokens = (
        (grad_hidden + grad_x_norm).astype(jnp.bfloat16).reshape(shard_count, unit_max, width)
    )
    returned = lax.all_to_all(grad_tokens, "shard", split_axis=0, concat_axis=0, tiled=True)
    home_rows = (
        jnp.zeros(local_rows.shape, jnp.float32)
        .at[row_index]
        .add(jnp.where(sent_live[:, :, None], returned.astype(jnp.float32), 0.0))
    )
    grad_x = home_rows.astype(jnp.bfloat16)[None]
    attn_share = (
        lax.psum_scatter(
            grad_wq.astype(jnp.bfloat16), "shard", scatter_dimension=0, tiled=True
        ).astype(jnp.float32),
        lax.psum_scatter(
            grad_wk.astype(jnp.bfloat16), "shard", scatter_dimension=0, tiled=True
        ).astype(jnp.float32),
        lax.psum_scatter(
            grad_wv.astype(jnp.bfloat16), "shard", scatter_dimension=0, tiled=True
        ).astype(jnp.float32),
        lax.psum_scatter(
            grad_wo.astype(jnp.bfloat16), "shard", scatter_dimension=0, tiled=True
        ).astype(jnp.float32),
        lax.psum_scatter(
            grad_gain_one.astype(jnp.bfloat16), "shard", scatter_dimension=0, tiled=True
        ).astype(jnp.float32),
    )
    totals = (
        lax.psum(ffn_share[0].astype(jnp.bfloat16), "replica").astype(jnp.float32),
        lax.psum(ffn_share[1].astype(jnp.bfloat16), "replica").astype(jnp.float32),
        lax.psum(ffn_share[2].astype(jnp.bfloat16), "replica").astype(jnp.float32),
        lax.psum(ffn_share[3].astype(jnp.bfloat16), "replica").astype(jnp.float32),
        lax.psum(attn_share[0].astype(jnp.bfloat16), "replica").astype(jnp.float32),
        lax.psum(attn_share[1].astype(jnp.bfloat16), "replica").astype(jnp.float32),
        lax.psum(attn_share[2].astype(jnp.bfloat16), "replica").astype(jnp.float32),
        lax.psum(attn_share[3].astype(jnp.bfloat16), "replica").astype(jnp.float32),
        lax.psum(attn_share[4].astype(jnp.bfloat16), "replica").astype(jnp.float32),
    )
    return (
        layer_out,
        grad_x,
        totals[8],
        totals[3],
        totals[4],
        totals[5],
        totals[6],
        totals[7],
        totals[0],
        totals[1],
        totals[2],
    )


def solution(mesh):
    return jax.shard_map(
        shards,
        mesh=mesh,
        in_specs=(
            P("replica", "shard", None),
            P("replica", None),
            P("replica", None),
            P(),
            P("shard", None),
            P("shard", None),
            P("shard", None),
            P("shard", None),
            P(),
            P("shard", None),
            P("shard", None),
            P("shard", None),
            P("replica", "shard", None, None),
        ),
        out_specs=(
            P("replica", "shard", None, None),
            P("replica", "shard", None),
            P("shard"),
            P("shard"),
            P("shard", None),
            P("shard", None),
            P("shard", None),
            P("shard", None),
            P("shard", None),
            P("shard", None),
            P("shard", None),
        ),
        check_vma=False,
    )
```

profile of v0, /device:TPU:0, one launch (start us, length us, event | category | flops | bytes accessed | tf_op | source)
XLA Modules:
  0.0 894.3 jit_solution(441610172667195544)
XLA Ops:
  20.3 7.5 all-to-all-start
  29.4 35.4 %all-to-all-done = bf16[16,64,768]{2,1,0:T(8,128)(2,1)S(1)} async-done(((bf16[16,64,768]{2,1,0:T(8,128)(2,1)}), bf16[16,64,768]{2,1,0:T(8,128)(2,1)S(1)}, u32[]{:S(2)}, u32[]{:S(2)}) %all-to-all-start) | async-done | bytes 1572896 | tf_op jit(solution)/shard_map/all_to_all | solution.py:150
  70.1 33.1 %all-gather.12.cloned.1.call-done = bf16[768,768]{1,0:T(8,128)(2,1)} async-done(((bf16[48,768]{1,0:T(8,128)(2,1)}), bf16[768,768]{1,0:T(8,128)(2,1)}) %all-gather.12.cloned.1.call-update) | async-done | bytes 1179664 | tf_op jit(solution)/shard_map/all_gather | solution.py:157
  106.5 10.7 %fusion.65 = f32[12,512,1024]{2,1,0:T(8,128)} fusion(bf16[512,12,64]{0,2,1:T(8,128)(2,1)S(1)} %bitcast.124, bf16[1024,12,64]{0,2,1:T(8,128)(2,1)S(1)} %bitcast.120), kind=kOutput, calls=%fused_computation.130 | convolution fusion | flops 805306368 | bytes 27525120 | tf_op jit(solution)/shard_map/qhd,khd->hqk/dot_general | solution.py:53
  117.2 16.7 %fusion.12 = (f32[12,512]{1,0:T(8,128)S(1)}, f32[12,512]{1,0:T(8,128)S(1)}, f32[12,512,1024]{2,1,0:T(8,128)}) fusion(pred[1024]{0:T(1024)(128)(4,1)S(1)} %broadcast_in_dim.135, f32[12,512,1024]{2,1,0:T(8,128)} %fusion.65, bf16[512,12,64]{0,2,1:T(8,128)(2,1)S(1)} %bitcast.130, bf16[1024,12,64]{0,2,1:T(8,128)(2,1)} %bitcast.121), kind=kOutput, calls=%fused_computation.26 | convolution fusion | flops 843042816 | bytes 52741120 | tf_op jit(solution)/shard_map/qhd,khd->hqk/dot_general | solution.py:53
  133.9 18.7 %fusion = (f32[12,512]{1,0:T(8,128)S(1)}, f32[12,512]{1,0:T(8,128)S(1)}) fusion(f32[12,512]{1,0:T(8,128)S(1)} %get-tuple-element.19, f32[12,512,1024]{2,1,0:T(8,128)} %get-tuple-element.47, pred[1024]{0:T(1024)(128)(4,1)S(1)} %broadcast_in_dim.135, f32[12,512]{1,0:T(8,128)S(1)} %get-tuple-element.20, f32[12,512,1024]{2,1,0:T(8,128)} %fusion.65), kind=kLoop, calls=%fused_computation.14 | loop fusion | flops 50319360 | bytes 50430976 | tf_op jit(solution)/shard_map/reduce_sum | solution.py:59
  155.8 11.7 %fusion.37 = bf16[12,64,512]{2,1,0:T(8,128)(2,1)S(1)} fusion(bf16[1024,12,64]{0,2,1:T(8,128)(2,1)S(1)} %bitcast.126, f32[12,512]{1,0:T(8,128)S(1)} %get-tuple-element.17, f32[12,512]{1,0:T(8,128)S(1)} %get-tuple-element.19, f32[12,512,1024]{2,1,0:T(8,128)} %get-tuple-element.47, pred[1024]{0:T(1024)(128)(4,1)S(1)} %broadcast_in_dim.135), kind=kOutput, calls=%fused_computation.87 | convolution fusion | flops 837156864 | bytes 27575296 | tf_op jit(solution)/shard_map/hqk,khd->qhd/dot_general | solution.py:61
  167.6 12.2 %fusion.36 = bf16[12,64,512]{2,1,0:T(8,128)(2,1)} fusion(bf16[1024,12,64]{0,2,1:T(8,128)(2,1)S(1)} %bitcast.127, f32[12,512]{1,0:T(8,128)S(1)} %get-tuple-element.18, f32[12,512]{1,0:T(8,128)S(1)} %get-tuple-element.20, f32[12,512,1024]{2,1,0:T(8,128)} %fusion.65, pred[1024]{0:T(1024)(128)(4,1)S(1)} %broadcast_in_dim.135), kind=kOutput, calls=%fused_computation.86 | convolution fusion | flops 837156864 | bytes 27575296 | tf_op jit(solution)/shard_map/hqk,khd->qhd/dot_general | solution.py:61
  187.8 40.9 %all-gather.18.cloned.1.call-done = bf16[768,2048]{1,0:T(8,128)(2,1)} async-done(((bf16[48,2048]{1,0:T(8,128)(2,1)}), bf16[768,2048]{1,0:T(8,128)(2,1)}) %all-gather.18.cloned.1.call-update) | async-done | bytes 3145744 | tf_op jit(solution)/shard_map/all_gather | solution.py:172
  228.7 7.5 fusion.67
  236.1 38.5 %all-gather.16.cloned.1.call-done = bf16[768,2048]{1,0:T(8,128)(2,1)} async-done(((bf16[48,2048]{1,0:T(8,128)(2,1)}), bf16[768,2048]{1,0:T(8,128)(2,1)}) %all-gather.16.cloned.1.call-update) | async-done | bytes 3145744 | tf_op jit(solution)/shard_map/all_gather | solution.py:171
  274.7 9.0 %fusion.66 = f32[1024,2048]{1,0:T(8,128)} fusion(bf16[1024,768]{1,0:T(8,128)(2,1)} %copy-done.22, bf16[768,2048]{1,0:T(8,128)(2,1)} %all-gather.16.cloned.1.call-done), kind=kOutput, calls=%fused_computation.131 | convolution fusion | flops 3221225472 | bytes 13107200 | tf_op jit(solution)/shard_map/dot_general | solution.py:39
  283.7 37.1 %all-gather.20.cloned.1.call-done = bf16[2048,768]{1,0:T(8,128)(2,1)} async-done(((bf16[128,768]{1,0:T(8,128)(2,1)}), bf16[2048,768]{1,0:T(8,128)(2,1)}) %all-gather.20.cloned.1.call-update) | async-done | bytes 3145744 | tf_op jit(solution)/shard_map/all_gather | solution.py:173
  320.8 15.1 %multiply_convert_fusion.2 = (bf16[1024,2048]{1,0:T(8,128)(2,1)S(1)}, bf16[1024,2048]{1,0:T(8,128)(2,1)}, bf16[1024,2048]{1,0:T(8,128)(2,1)}) fusion(f32[1024,2048]{1,0:T(8,128)} %fusion.66, f32[1024,2048]{1,0:T(8,128)} %fusion.67, bf16[2048,768]{1,0:T(8,128)(2,1)} %all-gather.20.cloned.1.call-done, bf16[1,1,1024,768]{3,2,1,0:T(8,128)(2,1)S(1)} %copy-done.16, ...), kind=kOutput, calls=%fused_computation.35 | convolution fusion | flops 3278110720 | bytes 34079744 | tf_op jit(solution)/shard_map/dot_general | solution.py:33
  335.9 7.3 fusion.68
  358.1 10.8 %fusion.69 = f32[12,512,1024]{2,1,0:T(8,128)} fusion(bf16[512,12,64]{0,2,1:T(8,128)(2,1)S(1)} %bitcast.132, bf16[1024,12,64]{0,2,1:T(8,128)(2,1)S(1)} %bitcast.128), kind=kOutput, calls=%fused_computation.134 | convolution fusion | flops 805306368 | bytes 27525120 | tf_op jit(solution)/shard_map/qhd,khd->hqk/dot_general | solution.py:87
  368.9 12.6 %fusion.4 = f32[12,64,1024]{2,1,0:T(8,128)} fusion(bf16[512,12,64]{0,2,1:T(8,128)(2,1)S(1)} %bitcast.133, f32[12,512]{1,0:T(8,128)S(1)} %get-tuple-element.53, f32[12,512,1024]{2,1,0:T(8,128)} %fusion.65, pred[1024]{0:T(1024)(128)(4,1)S(1)} %broadcast_in_dim.135), kind=kOutput, calls=%fused_computation.18 | convolution fusion | flops 830472192 | bytes 29123584 | tf_op jit(solution)/shard_map/hqk,qhd->khd/dot_general | solution.py:104
  381.5 35.6 %multiply_reduce_fusion.1 = (f32[12,512]{1,0:T(8,128)S(1)}, f32[12,512]{1,0:T(8,128)S(1)}, f32[12,512,1024]{2,1,0:T(8,128)}) fusion(f32[12,512]{1,0:T(8,128)S(1)} %get-tuple-element.54, f32[12,512,1024]{2,1,0:T(8,128)} %get-tuple-element.47, pred[1024]{0:T(1024)(128)(4,1)S(1)} %broadcast_in_dim.135, f32[12,512,1024]{2,1,0:T(8,128)} %fusion.69, ...), kind=kOutput, calls=%fused_computation.6 | convolution fusion | flops 868208640 | bytes 103121920 | tf_op jit(solution)/shard_map/qhd,khd->hqk/dot_general | solution.py:87
  417.1 12.3 %add_convert_fusion = bf16[12,64,1024]{2,1,0:T(8,128)(2,1)S(1)} fusion(f32[12,64,1024]{2,1,0:T(8,128)} %fusion.4, bf16[512,12,64]{0,2,1:T(8,128)(2,1)S(1)} %bitcast.138, f32[12,512]{1,0:T(8,128)S(1)} %get-tuple-element.54, f32[12,512,1024]{2,1,0:T(8,128)} %get-tuple-element.47, pred[1024]{0:T(1024)(128)(4,1)S(1)} %broadcast_in_dim.135), kind=kOutput, calls=%fused_computation.64 | convolution fusion | flops 832045056 | bytes 30696448 | tf_op jit(solution)/shard_map/hqk,qhd->khd/dot_general | solution.py:104
  433.1 42.5 %multiply_convert_fusion.1 = (bf16[12,512,1024]{2,1,0:T(8,128)(2,1)}, bf16[12,512,1024]{2,1,0:T(8,128)(2,1)}) fusion(f32[12,512,1024]{2,1,0:T(8,128)} %get-tuple-element.51, f32[12,512]{1,0:T(8,128)S(1)} %get-tuple-element.15, f32[12,512]{1,0:T(8,128)S(1)} %get-tuple-element.54, f32[12,512,1024]{2,1,0:T(8,128)} %get-tuple-element.47, ...), kind=kLoop, calls=%fused_computation.5 | loop fusion | flops 75497472 | bytes 125928448 | tf_op jit(solution)/shard_map/convert_element_type | solution.py:91
  475.7 8.6 multiply_convert_fusion.7
  484.3 8.7 multiply_convert_fusion.6
  512.5 7.9 convolution_convert_fusion
  520.5 7.9 convolution_convert_fusion.2
  528.8 7.8 convolution_convert_fusion.1
  552.7 60.4 %reduce-scatter.10.cloned.1.call-done = bf16[48,768]{1,0:T(8,128)(2,1)} async-done(((bf16[768,768]{1,0:T(8,128)(2,1)}), bf16[48,768]{1,0:T(8,128)(2,1)}) %reduce-scatter.10.cloned.1.call-update) | async-done | bytes 73744 | tf_op jit(solution)/shard_map/reduce_scatter | solution.py:250
  613.1 69.0 %reduce-scatter.20.cloned.1.call-done = bf16[128,768]{1,0:T(8,128)(2,1)} async-done(((bf16[2048,768]{1,0:T(8,128)(2,1)}), bf16[128,768]{1,0:T(8,128)(2,1)}) %reduce-scatter.20.cloned.1.call-update) | async-done | bytes 196624 | tf_op jit(solution)/shard_map/reduce_scatter | solution.py:206
  682.2 69.1 %reduce-scatter.16.cloned.1.call-done = bf16[48,2048]{1,0:T(8,128)(2,1)} async-done(((bf16[768,2048]{1,0:T(8,128)(2,1)}), bf16[48,2048]{1,0:T(8,128)(2,1)}) %reduce-scatter.16.cloned.1.call-update) | async-done | bytes 196624 | tf_op jit(solution)/shard_map/reduce_scatter | solution.py:200
  751.3 69.1 %reduce-scatter.18.cloned.1.call-done = bf16[48,2048]{1,0:T(8,128)(2,1)} async-done(((bf16[768,2048]{1,0:T(8,128)(2,1)}), bf16[48,2048]{1,0:T(8,128)(2,1)}) %reduce-scatter.18.cloned.1.call-update) | async-done | bytes 196624 | tf_op jit(solution)/shard_map/reduce_scatter | solution.py:203
  820.5 8.6 fusion.35
  829.1 29.5 %all-reduce.2 = (bf16[768]{0:T(1024)(128)(2,1)S(1)}, bf16[768]{0:T(1024)(128)(2,1)S(1)}) all-reduce(bf16[768]{0:T(1024)(128)(2,1)S(1)} %get-tuple-element.13, bf16[768]{0:T(1024)(128)(2,1)S(1)} %copy-done.36), channel_id=2, replica_groups=mesh['shard'=16,'replica'=2] {'shard'}, use_global_device_ids=true, to_apply=%region_16.17.clone | all-reduce | flops 1536 | bytes 6144
  866.7 8.6 scatter_custom_fusion
  (185 shorter events, 108.5 us)
Async XLA Ops:
  7.2 59.6 %all-gather.10.cloned.1.call-start = ((), (), s32[]{:S(2)}) async-start(), calls=%async_computation.10 | async-start | bytes 1253376 | tf_op jit(solution)/shard_map/all_gather | solution.py:156
  7.9 95.3 %all-gather.12.cloned.1.call-start = ((), (), s32[]{:S(2)}) async-start(), calls=%async_computation.11 | async-start | bytes 1253376 | tf_op jit(solution)/shard_map/all_gather | solution.py:157
  8.7 143.9 %all-gather.8.cloned.1.call-start = ((), (), s32[]{:S(2)}) async-start(), calls=%async_computation.9 | async-start | bytes 1253376 | tf_op jit(solution)/shard_map/all_gather | solution.py:158
  9.4 172.7 %all-gather.14.cloned.1.call-start = ((), (), s32[]{:S(2)}) async-start(), calls=%async_computation.12 | async-start | bytes 1253376 | tf_op jit(solution)/shard_map/all_gather | solution.py:159
  10.0 218.7 %all-gather.18.cloned.1.call-start = ((), (), s32[]{:S(2)}) async-start(), calls=%async_computation.14 | async-start | bytes 3342336 | tf_op jit(solution)/shard_map/all_gather | solution.py:172
  10.6 264.1 %all-gather.16.cloned.1.call-start = ((), (), s32[]{:S(2)}) async-start(), calls=%async_computation.13 | async-start | bytes 3342336 | tf_op jit(solution)/shard_map/all_gather | solution.py:171
  20.3 44.9 %copy-start.26 = (f32[768]{0:T(1024)S(1)}, f32[768]{0:T(1024)}, u32[]{:S(2)}) copy-start(f32[768]{0:T(1024)} %param.16) | copy-start | bytes 9220
  20.3 44.4 %all-to-all-start = ((bf16[16,64,768]{2,1,0:T(8,128)(2,1)}), bf16[16,64,768]{2,1,0:T(8,128)(2,1)S(1)}, u32[]{:S(2)}, u32[]{:S(2)}) async-start(bf16[16,64,768]{2,1,0:T(8,128)(2,1)} %broadcast_select_fusion), calls=%async_computation | async-start | bytes 3145728 | tf_op jit(solution)/shard_map/all_to_all | solution.py:150
  27.9 292.9 %all-gather.20.cloned.1.call-start = ((), (), s32[]{:S(2)}) async-start(), calls=%async_computation.15 | async-start | bytes 3342336 | tf_op jit(solution)/shard_map/all_gather | solution.py:173
  28.6 524.1 %reduce-scatter.14.cloned.1.call-start = ((), (), s32[]{:S(2)}) async-start(), calls=%async_computation.19 | async-start | bytes 1253376 | tf_op jit(solution)/shard_map/reduce_scatter | solution.py:256
  64.8 120.6 %copy-start.2 = (bf16[16,64,768]{2,1,0:T(8,128)(2,1)}, bf16[16,64,768]{2,1,0:T(8,128)(2,1)S(1)}, u32[]{:S(2)}) copy-start(bf16[16,64,768]{2,1,0:T(8,128)(2,1)S(1)} %all-to-all-done) | copy-start | bytes 4718596
  70.1 36.3 %copy-start.6 = (bf16[512,768]{0,1:T(8,128)(2,1)}, bf16[512,768]{0,1:T(8,128)(2,1)S(1)}, u32[]{:S(2)}) copy-start(bf16[512,768]{0,1:T(8,128)(2,1)S(1)} %get-tuple-element.39) | copy-start | bytes 2359300
  70.1 47.1 %copy-start.14 = (bf16[512,768]{0,1:T(8,128)(2,1)}, bf16[512,768]{0,1:T(8,128)(2,1)S(1)}, u32[]{:S(2)}) copy-start(bf16[512,768]{0,1:T(8,128)(2,1)S(1)} %get-tuple-element.40) | copy-start | bytes 2359300
  106.5 10.8 %copy-start.4 = (bf16[1024,768]{0,1:T(8,128)(2,1)}, bf16[1024,768]{0,1:T(8,128)(2,1)S(1)}, u32[]{:S(2)}) copy-start(bf16[1024,768]{0,1:T(8,128)(2,1)S(1)} %convolution_convert_fusion.4) | copy-start | bytes 4718596
  155.8 11.7 %copy-start.8 = (bf16[1024,768]{0,1:T(8,128)(2,1)}, bf16[1024,768]{0,1:T(8,128)(2,1)S(1)}, u32[]{:S(2)}) copy-start(bf16[1024,768]{0,1:T(8,128)(2,1)S(1)} %convolution_convert_fusion.6) | copy-start | bytes 4718596
  187.8 40.9 %copy-start.22 = (bf16[1024,768]{1,0:T(8,128)(2,1)}, bf16[1024,768]{1,0:T(8,128)(2,1)S(1)}, u32[]{:S(2)}) copy-start(bf16[1024,768]{1,0:T(8,128)(2,1)S(1)} %multiply_convert_fusion.5) | copy-start | bytes 4718596
  236.1 84.7 %copy-start.16 = (bf16[1,1,1024,768]{3,2,1,0:T(8,128)(2,1)S(1)}, bf16[1,1,1024,768]{3,2,1,0:T(8,128)(2,1)}, u32[]{:S(2)}) copy-start(bf16[1,1,1024,768]{3,2,1,0:T(8,128)(2,1)} %param.25) | copy-start | bytes 4718596
  320.8 15.1 %copy-start.38 = (bf16[768,2048]{1,0:T(8,128)(2,1)S(1)}, bf16[768,2048]{1,0:T(8,128)(2,1)}, u32[]{:S(2)}) copy-start(bf16[768,2048]{1,0:T(8,128)(2,1)} %all-gather.16.cloned.1.call-done) | copy-start | bytes 9437188
  353.3 199.4 %reduce-scatter.12.cloned.1.call-start = ((), (), s32[]{:S(2)}) async-start(), calls=%async_computation.18 | async-start | bytes 1253376 | tf_op jit(solution)/shard_map/reduce_scatter | solution.py:253
  417.1 13.5 %copy-start.20 = (bf16[16,64,768]{2,1,0:T(8,128)(2,1)S(1)}, bf16[16,64,768]{2,1,0:T(8,128)(2,1)}, u32[]{:S(2)}) copy-start(bf16[16,64,768]{2,1,0:T(8,128)(2,1)} %fusion.31) | copy-start | bytes 4718596
  433.1 119.6 %reduce-scatter.8.cloned.1.call-start = ((), (), s32[]{:S(2)}) async-start(), calls=%async_computation.16 | async-start | bytes 1253376 | tf_op jit(solution)/shard_map/reduce_scatter | solution.py:247
  433.1 42.6 %copy-start.5 = (bf16[1024,768]{0,1:T(8,128)(2,1)S(1)}, bf16[1024,768]{0,1:T(8,128)(2,1)}, u32[]{:S(2)}) copy-start(bf16[1024,768]{0,1:T(8,128)(2,1)} %copy-done.4) | copy-start | bytes 4718596
  484.3 8.7 copy-start.19
  495.4 117.7 %reduce-scatter.10.cloned.1.call-start = ((), (), s32[]{:S(2)}) async-start(), calls=%async_computation.17 | async-start | bytes 1253376 | tf_op jit(solution)/shard_map/reduce_scatter | solution.py:250
  512.4 169.8 %reduce-scatter.20.cloned.1.call-start = ((), (), s32[]{:S(2)}) async-start(), calls=%async_computation.22 | async-start | bytes 3342336 | tf_op jit(solution)/shard_map/reduce_scatter | solution.py:206
  520.4 230.9 %reduce-scatter.16.cloned.1.call-start = ((), (), s32[]{:S(2)}) async-start(), calls=%async_computation.20 | async-start | bytes 3342336 | tf_op jit(solution)/shard_map/reduce_scatter | solution.py:200
  528.4 292.1 %reduce-scatter.18.cloned.1.call-start = ((), (), s32[]{:S(2)}) async-start(), calls=%async_computation.21 | async-start | bytes 3342336 | tf_op jit(solution)/shard_map/reduce_scatter | solution.py:203
  547.3 317.4 %all-to-all-start.1 = ((bf16[16,64,768]{2,1,0:T(8,128)(2,1)}), bf16[16,64,768]{2,1,0:T(8,128)(2,1)S(1)}, u32[]{:S(2)}, u32[]{:S(2)}) async-start(bf16[16,64,768]{2,1,0:T(8,128)(2,1)} %bitcast.26), calls=%async_computation.1 | async-start | bytes 3145728 | tf_op jit(solution)/shard_map/all_to_all | solution.py:239
  551.2 325.1 %all-reduce.7.cloned.1.call-start = ((), (), s32[]{:S(2)}) async-start(), calls=%async_computation.23 | async-start | bytes 1769472 | tf_op jit(solution)/shard_map/psum | solution.py:268
  820.5 8.6 copy-start.36
  820.5 44.2 %copy-start.33 = (pred[16,64]{1,0:T(8,128)(4,1)S(1)}, pred[16,64]{1,0:T(8,128)(4,1)}, u32[]{:S(2)}) copy-start(pred[16,64]{1,0:T(8,128)(4,1)} %copy-done.32) | copy-start | bytes 3076
  866.7 20.9 %copy-start.1 = (bf16[1,512,768]{2,1,0:T(8,128)(2,1)S(1)}, bf16[1,512,768]{2,1,0:T(8,128)(2,1)}, u32[]{:S(2)}) copy-start(bf16[1,512,768]{2,1,0:T(8,128)(2,1)} %param.13) | copy-start | bytes 2359300
  (29 other events, 91.8 us)
Sparse Core Ops, SparseCore 0:
  10.3 51.5 all-gather.9
  64.1 39.0 all-gather.11
  105.6 37.1 all-gather.7
  144.9 37.1 all-gather.13
  184.2 44.3 all-gather.17
  230.8 43.8 all-gather.15
  276.9 43.8 all-gather.19
  353.5 56.5 reduce-scatter.13
  433.2 56.6 reduce-scatter.11
  495.5 56.5 reduce-scatter.7
  555.8 57.3 reduce-scatter.9
  616.8 65.3 reduce-scatter.19
  686.0 65.2 reduce-scatter.15
  755.0 65.4 reduce-scatter.17
  823.0 35.4 all-reduce.6
where the time goes:
time: 900 us; the launch traced here: 894 us
  waiting for transfers between devices  460 us (51%)
  matrix products  262 us (29%)
  other arithmetic  97.7 us (11%)
  blocking collectives  34.4 us (4%)
  between operations  15.4 us (2%)
  starting transfers between devices  12.7 us (1%)
  local copies, waits for them, and re-layouts  12.1 us (1%)
    reduce_scatter x1, waiting for transfers between devices, shards(): lax.psum_scatter(grad_wg.astype(jnp.bfloat16), 'shard', scatter_dimension...  69.1 us
    reduce_scatter x1, waiting for transfers between devices, shards(): lax.psum_scatter(grad_wu.astype(jnp.bfloat16), 'shard', scatter_dimension...  69.1 us
    reduce_scatter x1, waiting for transfers between devices, shards(): lax.psum_scatter(grad_down.astype(jnp.bfloat16), 'shard', scatter_dimensi...  69 us
    reduce_scatter x1, waiting for transfers between devices, shards(): lax.psum_scatter(grad_wk.astype(jnp.bfloat16), 'shard', scatter_dimension...  60.4 us
    dot_general x2, matrix products, attend_backward(): jnp.einsum('qhd,khd->hqk', grad_heads, value_heads, preferred_element_typ...  46.4 us
    convert_element_type x1, other arithmetic, attend_backward(): grad_scores = (prob_vals * (grad_probs - row_dot)).astype(jnp.bfloat16)  42.5 us
    all_gather x1, waiting for transfers between devices, shards(): lax.all_gather(w_up, 'shard', axis=0, tiled=True)  40.9 us
    all_gather x1, waiting for transfers between devices, shards(): lax.all_gather(w_gate, 'shard', axis=0, tiled=True)  38.5 us
  transfers between devices with their start and end apart: 17, of which 10 were waited for; matrix products, arithmetic and copies ran while one was open for 36% of the time, Pallas kernels for 0%

commit v1 on v0

--- a/solution.py
+++ b/solution.py
@@ -1,3 +1,4 @@
+import functools
 import jax
 import jax.numpy as jnp
 from jax import lax
@@ -7,6 +8,31 @@
 HD = 64
 norm_eps = 1e-06
 neg_big = -1e30
+
+
+def spread_files(state, group_axis, k_dim):
+    carry, x_next, current_arr = (
+        lax.axis_size(group_axis),
+        lax.axis_index(group_axis),
+        state.shape[k_dim],
+    )
+    local_now, g_now = (state, 1)
+    while g_now < carry:
+        local_now = jnp.concatenate(
+            [
+                local_now,
+                lax.ppermute(
+                    local_now, group_axis, [(idx, (idx - g_now) % carry) for idx in range(carry)]
+                ),
+            ],
+            axis=k_dim,
+        )
+        g_now = 2 * g_now
+    moved = jnp.roll(local_now, x_next * current_arr, axis=k_dim)
+    return moved
+
+
+lift_stacks_all = functools.partial(spread_files, group_axis="shard", k_dim=0)
 
 
 def rms_scale(tok_rows, gain_vec):
@@ -170,7 +196,7 @@
     wg_full, wu_full, wd_full = (
         lax.all_gather(w_gate, "shard", axis=0, tiled=True),
         lax.all_gather(w_up, "shard", axis=0, tiled=True),
-        lax.all_gather(w_down, "shard", axis=0, tiled=True),
+        lift_stacks_all(w_down),
     )
     normed_two_f, norm_two_back = jax.vjp(rms_scale, hidden_res, gain_ffn)
     normed_two = normed_two_f.astype(jnp.bfloat16)

time: 900 us -> 954 us (1.060)
  waiting for transfers between devices: 460 us -> 493 us
  local copies, waits for them, and re-layouts: 12.1 us -> 24 us
    ppermute x0 -> x4, waiting for transfers between devices: none -> 101 us  [spread_files(): lax.ppermute(local_now, group_axis, [(idx, (idx - g_now) % carry) for idx...]
    reduce_scatter x1, waiting for transfers between devices: 60.4 us -> 0.01 us  [shards(): lax.psum_scatter(grad_wk.astype(jnp.bfloat16), 'shard', scatter_dimension...]
    unnamed x91 -> x110, local copies, waits for them, and re-layouts: 7.63 us -> 18.2 us
  transfers between devices with their start and end apart: 17 -> 21, of which waited for: 10 -> 13; matrix products, arithmetic and copies ran while one was open for 36% -> 35% of each run, Pallas kernels for 0% -> 0%
where the time goes in v1:
time: 954 us; the launch traced here: 949 us
  waiting for transfers between devices  493 us (52%)
  matrix products  261 us (27%)
  other arithmetic  101 us (11%)
  blocking collectives  34.7 us (4%)
  local copies, waits for them, and re-layouts  24 us (3%)
  starting transfers between devices  19.4 us (2%)
  between operations  15.7 us (2%)
    ppermute x4, waiting for transfers between devices, spread_files(): lax.ppermute(local_now, group_axis, [(idx, (idx - g_now) % carry) for idx...  101 us
    reduce_scatter x1, waiting for transfers between devices, shards(): lax.psum_scatter(grad_wg.astype(jnp.bfloat16), 'shard', scatter_dimension...  69.1 us
    reduce_scatter x1, waiting for transfers between devices, shards(): lax.psum_scatter(grad_wu.astype(jnp.bfloat16), 'shard', scatter_dimension...  69 us
    reduce_scatter x1, waiting for transfers between devices, shards(): lax.psum_scatter(grad_down.astype(jnp.bfloat16), 'shard', scatter_dimensi...  62.3 us
    dot_general x2, matrix products, attend_backward(): jnp.einsum('qhd,khd->hqk', grad_heads, value_heads, preferred_element_typ...  46.4 us
    convert_element_type x1, other arithmetic, attend_backward(): grad_scores = (prob_vals * (grad_probs - row_dot)).astype(jnp.bfloat16)  42.5 us
    all_gather x1, waiting for transfers between devices, shards(): lax.all_gather(w_up, 'shard', axis=0, tiled=True)  40.9 us
    all_gather x1, waiting for transfers between devices, shards(): lax.all_gather(w_gate, 'shard', axis=0, tiled=True)  38.5 us
  transfers between devices with their start and end apart: 21, of which 13 were waited for; matrix products, arithmetic and copies ran while one was open for 35% of the time, Pallas kernels for 0%

profile of v1, /device:TPU:0, one launch (start us, length us, event | category | flops | bytes accessed | tf_op | source)
XLA Modules:
  0.0 949.2 jit_solution(3864429193989277587)
XLA Ops:
  20.3 7.5 all-to-all-start
  29.4 35.4 %all-to-all-done = bf16[16,64,768]{2,1,0:T(8,128)(2,1)S(1)} async-done(((bf16[16,64,768]{2,1,0:T(8,128)(2,1)}), bf16[16,64,768]{2,1,0:T(8,128)(2,1)S(1)}, u32[]{:S(2)}, u32[]{:S(2)}) %all-to-all-start) | async-done | bytes 1572896 | tf_op jit(solution)/shard_map/all_to_all | solution.py:176
  70.1 33.1 %all-gather.12.cloned.1.call-done = bf16[768,768]{1,0:T(8,128)(2,1)} async-done(((bf16[48,768]{1,0:T(8,128)(2,1)}), bf16[768,768]{1,0:T(8,128)(2,1)}) %all-gather.12.cloned.1.call-update) | async-done | bytes 1179664 | tf_op jit(solution)/shard_map/all_gather | solution.py:183
  106.5 10.7 %fusion.70 = f32[12,512,1024]{2,1,0:T(8,128)} fusion(bf16[512,12,64]{0,2,1:T(8,128)(2,1)S(1)} %bitcast.123, bf16[1024,12,64]{0,2,1:T(8,128)(2,1)S(1)} %bitcast.119), kind=kOutput, calls=%fused_computation.146 | convolution fusion | flops 805306368 | bytes 27525120 | tf_op jit(solution)/shard_map/qhd,khd->hqk/dot_general | solution.py:79
  117.2 16.7 %fusion.12 = (f32[12,512]{1,0:T(8,128)S(1)}, f32[12,512]{1,0:T(8,128)S(1)}, f32[12,512,1024]{2,1,0:T(8,128)}) fusion(pred[1024]{0:T(1024)(128)(4,1)S(1)} %broadcast_in_dim.135, f32[12,512,1024]{2,1,0:T(8,128)} %fusion.70, bf16[512,12,64]{0,2,1:T(8,128)(2,1)S(1)} %bitcast.129, bf16[1024,12,64]{0,2,1:T(8,128)(2,1)} %bitcast.120), kind=kOutput, calls=%fused_computation.26 | convolution fusion | flops 843042816 | bytes 52741120 | tf_op jit(solution)/shard_map/qhd,khd->hqk/dot_general | solution.py:79
  133.9 18.7 %fusion = (f32[12,512]{1,0:T(8,128)S(1)}, f32[12,512]{1,0:T(8,128)S(1)}) fusion(f32[12,512]{1,0:T(8,128)S(1)} %get-tuple-element.19, f32[12,512,1024]{2,1,0:T(8,128)} %get-tuple-element.47, pred[1024]{0:T(1024)(128)(4,1)S(1)} %broadcast_in_dim.135, f32[12,512]{1,0:T(8,128)S(1)} %get-tuple-element.20, f32[12,512,1024]{2,1,0:T(8,128)} %fusion.70), kind=kLoop, calls=%fused_computation.14 | loop fusion | flops 50319360 | bytes 50430976 | tf_op jit(solution)/shard_map/reduce_sum | solution.py:85
  155.8 11.7 %fusion.39 = bf16[12,64,512]{2,1,0:T(8,128)(2,1)S(1)} fusion(bf16[1024,12,64]{0,2,1:T(8,128)(2,1)S(1)} %bitcast.125, f32[12,512]{1,0:T(8,128)S(1)} %get-tuple-element.17, f32[12,512]{1,0:T(8,128)S(1)} %get-tuple-element.19, f32[12,512,1024]{2,1,0:T(8,128)} %get-tuple-element.47, pred[1024]{0:T(1024)(128)(4,1)S(1)} %broadcast_in_dim.135), kind=kOutput, calls=%fused_computation.90 | convolution fusion | flops 837156864 | bytes 27575296 | tf_op jit(solution)/shard_map/hqk,khd->qhd/dot_general | solution.py:87
  167.5 12.2 %fusion.38 = bf16[12,64,512]{2,1,0:T(8,128)(2,1)} fusion(bf16[1024,12,64]{0,2,1:T(8,128)(2,1)S(1)} %bitcast.126, f32[12,512]{1,0:T(8,128)S(1)} %get-tuple-element.18, f32[12,512]{1,0:T(8,128)S(1)} %get-tuple-element.20, f32[12,512,1024]{2,1,0:T(8,128)} %fusion.70, pred[1024]{0:T(1024)(128)(4,1)S(1)} %broadcast_in_dim.135), kind=kOutput, calls=%fused_computation.89 | convolution fusion | flops 837156864 | bytes 27575296 | tf_op jit(solution)/shard_map/hqk,khd->qhd/dot_general | solution.py:87
  187.8 40.9 %all-gather.18.cloned.1.call-done = bf16[768,2048]{1,0:T(8,128)(2,1)} async-done(((bf16[48,2048]{1,0:T(8,128)(2,1)}), bf16[768,2048]{1,0:T(8,128)(2,1)}) %all-gather.18.cloned.1.call-update) | async-done | bytes 3145744 | tf_op jit(solution)/shard_map/all_gather | solution.py:198
  228.7 7.5 fusion.72
  236.1 38.5 %all-gather.16.cloned.1.call-done = bf16[768,2048]{1,0:T(8,128)(2,1)} async-done(((bf16[48,2048]{1,0:T(8,128)(2,1)}), bf16[768,2048]{1,0:T(8,128)(2,1)}) %all-gather.16.cloned.1.call-update) | async-done | bytes 3145744 | tf_op jit(solution)/shard_map/all_gather | solution.py:197
  274.6 9.0 fusion.71
  283.7 37.1 %all-gather.20.cloned.1.call-done = bf16[2048,768]{1,0:T(8,128)(2,1)} async-done(((bf16[128,768]{1,0:T(8,128)(2,1)}), bf16[2048,768]{1,0:T(8,128)(2,1)}) %all-gather.20.cloned.1.call-update) | async-done | bytes 3145744 | tf_op jit(solution)/shard_map/all_gather | solution.py:212
  320.8 15.1 %multiply_convert_fusion.2 = (bf16[1024,2048]{1,0:T(8,128)(2,1)S(1)}, bf16[1024,2048]{1,0:T(8,128)(2,1)}, bf16[1024,2048]{1,0:T(8,128)(2,1)}) fusion(f32[1024,2048]{1,0:T(8,128)} %fusion.71, f32[1024,2048]{1,0:T(8,128)} %fusion.72, bf16[2048,768]{1,0:T(8,128)(2,1)} %all-gather.20.cloned.1.call-done, bf16[1,1,1024,768]{3,2,1,0:T(8,128)(2,1)S(1)} %copy-done.19, ...), kind=kOutput, calls=%fused_computation.35 | convolution fusion | flops 3278110720 | bytes 34079744 | tf_op jit(solution)/shard_map/dot_general | solution.py:59
  335.9 7.3 fusion.73
  358.1 10.8 %fusion.74 = f32[12,512,1024]{2,1,0:T(8,128)} fusion(bf16[512,12,64]{0,2,1:T(8,128)(2,1)S(1)} %bitcast.131, bf16[1024,12,64]{0,2,1:T(8,128)(2,1)S(1)} %bitcast.127), kind=kOutput, calls=%fused_computation.150 | convolution fusion | flops 805306368 | bytes 27525120 | tf_op jit(solution)/shard_map/qhd,khd->hqk/dot_general | solution.py:113
  368.9 12.6 %fusion.4 = f32[12,64,1024]{2,1,0:T(8,128)} fusion(bf16[512,12,64]{0,2,1:T(8,128)(2,1)S(1)} %bitcast.132, f32[12,512]{1,0:T(8,128)S(1)} %get-tuple-element.53, f32[12,512,1024]{2,1,0:T(8,128)} %fusion.70, pred[1024]{0:T(1024)(128)(4,1)S(1)} %broadcast_in_dim.135), kind=kOutput, calls=%fused_computation.18 | convolution fusion | flops 830472192 | bytes 29123584 | tf_op jit(solution)/shard_map/hqk,qhd->khd/dot_general | solution.py:130
  381.5 35.6 %multiply_reduce_fusion.1 = (f32[12,512]{1,0:T(8,128)S(1)}, f32[12,512]{1,0:T(8,128)S(1)}, f32[12,512,1024]{2,1,0:T(8,128)}) fusion(f32[12,512]{1,0:T(8,128)S(1)} %get-tuple-element.54, f32[12,512,1024]{2,1,0:T(8,128)} %get-tuple-element.47, pred[1024]{0:T(1024)(128)(4,1)S(1)} %broadcast_in_dim.135, f32[12,512,1024]{2,1,0:T(8,128)} %fusion.74, ...), kind=kOutput, calls=%fused_computation.6 | convolution fusion | flops 868208640 | bytes 103121920 | tf_op jit(solution)/shard_map/qhd,khd->hqk/dot_general | solution.py:113
  417.1 12.3 %add_convert_fusion = bf16[12,64,1024]{2,1,0:T(8,128)(2,1)S(1)} fusion(f32[12,64,1024]{2,1,0:T(8,128)} %fusion.4, bf16[512,12,64]{0,2,1:T(8,128)(2,1)S(1)} %bitcast.137, f32[12,512]{1,0:T(8,128)S(1)} %get-tuple-element.54, f32[12,512,1024]{2,1,0:T(8,128)} %get-tuple-element.47, pred[1024]{0:T(1024)(128)(4,1)S(1)} %broadcast_in_dim.135), kind=kOutput, calls=%fused_computation.64 | convolution fusion | flops 832045056 | bytes 30696448 | tf_op jit(solution)/shard_map/hqk,qhd->khd/dot_general | solution.py:130
  433.0 42.5 %multiply_convert_fusion.1 = (bf16[12,512,1024]{2,1,0:T(8,128)(2,1)}, bf16[12,512,1024]{2,1,0:T(8,128)(2,1)}) fusion(f32[12,512,1024]{2,1,0:T(8,128)} %get-tuple-element.51, f32[12,512]{1,0:T(8,128)S(1)} %get-tuple-element.15, f32[12,512]{1,0:T(8,128)S(1)} %get-tuple-element.54, f32[12,512,1024]{2,1,0:T(8,128)} %get-tuple-element.47, ...), kind=kLoop, calls=%fused_computation.5 | loop fusion | flops 75497472 | bytes 125928448 | tf_op jit(solution)/shard_map/convert_element_type | solution.py:117
  475.6 8.6 multiply_convert_fusion.7
  484.2 8.9 multiply_convert_fusion.6
  514.6 7.5 convolution_convert_fusion
  537.9 10.9 %collective-permute-done.1 = bf16[256,768]{1,0:T(8,128)(2,1)S(1)} collective-permute-done((bf16[256,768]{1,0:T(8,128)(2,1)S(1)}, bf16[256,768]{1,0:T(8,128)(2,1)S(1)}, u32[]{:S(2)}, u32[]{:S(2)}) %collective-permute-start.1) | collective-permute-done | bytes 393248 | tf_op jit(solution)/shard_map/ppermute | solution.py:24
  557.9 12.7 %collective-permute-done.2 = bf16[512,768]{1,0:T(8,128)(2,1)S(1)} collective-permute-done((bf16[512,768]{1,0:T(8,128)(2,1)}, bf16[512,768]{1,0:T(8,128)(2,1)S(1)}, u32[]{:S(2)}, u32[]{:S(2)}) %collective-permute-start.2) | collective-permute-done | bytes 786464 | tf_op jit(solution)/shard_map/ppermute | solution.py:24
  593.1 74.1 %collective-permute-done.3 = bf16[1024,768]{1,0:T(8,128)(2,1)S(1)} collective-permute-done((bf16[1024,768]{1,0:T(8,128)(2,1)}, bf16[1024,768]{1,0:T(8,128)(2,1)S(1)}, u32[]{:S(2)}, u32[]{:S(2)}) %collective-permute-start.3) | collective-permute-done | bytes 1572896 | tf_op jit(solution)/shard_map/ppermute | solution.py:24
  672.9 62.3 %reduce-scatter.20.cloned.1.call-done = bf16[128,768]{1,0:T(8,128)(2,1)} async-done(((bf16[2048,768]{1,0:T(8,128)(2,1)}), bf16[128,768]{1,0:T(8,128)(2,1)}) %reduce-scatter.20.cloned.1.call-update) | async-done | bytes 196624 | tf_op jit(solution)/shard_map/reduce_scatter | solution.py:232
  735.2 69.1 %reduce-scatter.16.cloned.1.call-done = bf16[48,2048]{1,0:T(8,128)(2,1)} async-done(((bf16[768,2048]{1,0:T(8,128)(2,1)}), bf16[48,2048]{1,0:T(8,128)(2,1)}) %reduce-scatter.16.cloned.1.call-update) | async-done | bytes 196624 | tf_op jit(solution)/shard_map/reduce_scatter | solution.py:226
  804.3 69.0 %reduce-scatter.18.cloned.1.call-done = bf16[48,2048]{1,0:T(8,128)(2,1)} async-done(((bf16[768,2048]{1,0:T(8,128)(2,1)}), bf16[48,2048]{1,0:T(8,128)(2,1)}) %reduce-scatter.18.cloned.1.call-update) | async-done | bytes 196624 | tf_op jit(solution)/shard_map/reduce_scatter | solution.py:229
  873.3 8.6 fusion.37
  881.9 29.5 %all-reduce.2 = (bf16[768]{0:T(1024)(128)(2,1)S(1)}, bf16[768]{0:T(1024)(128)(2,1)S(1)}) all-reduce(bf16[768]{0:T(1024)(128)(2,1)S(1)} %get-tuple-element.13, bf16[768]{0:T(1024)(128)(2,1)S(1)} %copy-done.41), channel_id=2, replica_groups=mesh['shard'=16,'replica'=2] {'shard'}, use_global_device_ids=true, to_apply=%region_16.17.clone | all-reduce | flops 1536 | bytes 6144
  921.2 8.6 scatter_custom_fusion
  (216 shorter events, 148.5 us)
Async XLA Ops:
  7.2 59.6 %all-gather.10.cloned.1.call-start = ((), (), s32[]{:S(2)}) async-start(), calls=%async_computation.10 | async-start | bytes 1253376 | tf_op jit(solution)/shard_map/all_gather | solution.py:182
  7.9 95.3 %all-gather.12.cloned.1.call-start = ((), (), s32[]{:S(2)}) async-start(), calls=%async_computation.11 | async-start | bytes 1253376 | tf_op jit(solution)/shard_map/all_gather | solution.py:183
  8.7 143.9 %all-gather.8.cloned.1.call-start = ((), (), s32[]{:S(2)}) async-start(), calls=%async_computation.9 | async-start | bytes 1253376 | tf_op jit(solution)/shard_map/all_gather | solution.py:184
  9.4 172.7 %all-gather.14.cloned.1.call-start = ((), (), s32[]{:S(2)}) async-start(), calls=%async_computation.12 | async-start | bytes 1253376 | tf_op jit(solution)/shard_map/all_gather | solution.py:185
  10.0 218.7 %all-gather.18.cloned.1.call-start = ((), (), s32[]{:S(2)}) async-start(), calls=%async_computation.14 | async-start | bytes 3342336 | tf_op jit(solution)/shard_map/all_gather | solution.py:198
  10.6 264.1 %all-gather.16.cloned.1.call-start = ((), (), s32[]{:S(2)}) async-start(), calls=%async_computation.13 | async-start | bytes 3342336 | tf_op jit(solution)/shard_map/all_gather | solution.py:197
  20.3 44.9 %copy-start.31 = (f32[768]{0:T(1024)S(1)}, f32[768]{0:T(1024)}, u32[]{:S(2)}) copy-start(f32[768]{0:T(1024)} %param.16) | copy-start | bytes 9220
  20.3 44.4 %all-to-all-start = ((bf16[16,64,768]{2,1,0:T(8,128)(2,1)}), bf16[16,64,768]{2,1,0:T(8,128)(2,1)S(1)}, u32[]{:S(2)}, u32[]{:S(2)}) async-start(bf16[16,64,768]{2,1,0:T(8,128)(2,1)} %broadcast_select_fusion), calls=%async_computation | async-start | bytes 3145728 | tf_op jit(solution)/shard_map/all_to_all | solution.py:176
  27.9 292.9 %all-gather.20.cloned.1.call-start = ((), (), s32[]{:S(2)}) async-start(), calls=%async_computation.15 | async-start | bytes 3342336 | tf_op jit(solution)/shard_map/all_gather | solution.py:212
  28.6 644.3 %reduce-scatter.14.cloned.1.call-start = ((), (), s32[]{:S(2)}) async-start(), calls=%async_computation.19 | async-start | bytes 1253376 | tf_op jit(solution)/shard_map/reduce_scatter | solution.py:282
  64.8 120.6 %copy-start.2 = (bf16[16,64,768]{2,1,0:T(8,128)(2,1)}, bf16[16,64,768]{2,1,0:T(8,128)(2,1)S(1)}, u32[]{:S(2)}) copy-start(bf16[16,64,768]{2,1,0:T(8,128)(2,1)S(1)} %all-to-all-done) | copy-start | bytes 4718596
  70.1 36.3 %copy-start.6 = (bf16[512,768]{0,1:T(8,128)(2,1)}, bf16[512,768]{0,1:T(8,128)(2,1)S(1)}, u32[]{:S(2)}) copy-start(bf16[512,768]{0,1:T(8,128)(2,1)S(1)} %get-tuple-element.39) | copy-start | bytes 2359300
  70.1 47.1 %copy-start.14 = (bf16[512,768]{0,1:T(8,128)(2,1)}, bf16[512,768]{0,1:T(8,128)(2,1)S(1)}, u32[]{:S(2)}) copy-start(bf16[512,768]{0,1:T(8,128)(2,1)S(1)} %get-tuple-element.40) | copy-start | bytes 2359300
  187.8 40.9 %copy-start.26 = (bf16[1024,768]{1,0:T(8,128)(2,1)}, bf16[1024,768]{1,0:T(8,128)(2,1)S(1)}, u32[]{:S(2)}) copy-start(bf16[1024,768]{1,0:T(8,128)(2,1)S(1)} %multiply_convert_fusion.5) | copy-start | bytes 4718596
  236.1 84.6 %copy-start.19 = (bf16[1,1,1024,768]{3,2,1,0:T(8,128)(2,1)S(1)}, bf16[1,1,1024,768]{3,2,1,0:T(8,128)(2,1)}, u32[]{:S(2)}) copy-start(bf16[1,1,1024,768]{3,2,1,0:T(8,128)(2,1)} %param.25) | copy-start | bytes 4718596
  320.8 15.1 %copy-start.43 = (bf16[768,2048]{1,0:T(8,128)(2,1)S(1)}, bf16[768,2048]{1,0:T(8,128)(2,1)}, u32[]{:S(2)}) copy-start(bf16[768,2048]{1,0:T(8,128)(2,1)} %all-gather.16.cloned.1.call-done) | copy-start | bytes 9437188
  353.3 319.6 %reduce-scatter.12.cloned.1.call-start = ((), (), s32[]{:S(2)}) async-start(), calls=%async_computation.18 | async-start | bytes 1253376 | tf_op jit(solution)/shard_map/reduce_scatter | solution.py:279
  417.1 13.4 %copy-start.24 = (bf16[16,64,768]{2,1,0:T(8,128)(2,1)S(1)}, bf16[16,64,768]{2,1,0:T(8,128)(2,1)}, u32[]{:S(2)}) copy-start(bf16[16,64,768]{2,1,0:T(8,128)(2,1)} %fusion.31) | copy-start | bytes 4718596
  433.0 239.9 %reduce-scatter.8.cloned.1.call-start = ((), (), s32[]{:S(2)}) async-start(), calls=%async_computation.16 | async-start | bytes 1253376 | tf_op jit(solution)/shard_map/reduce_scatter | solution.py:273
  433.0 42.6 %copy-start.5 = (bf16[1024,768]{0,1:T(8,128)(2,1)S(1)}, bf16[1024,768]{0,1:T(8,128)(2,1)}, u32[]{:S(2)}) copy-start(bf16[1024,768]{0,1:T(8,128)(2,1)} %copy-done.4) | copy-start | bytes 4718596
  496.4 176.5 %reduce-scatter.10.cloned.1.call-start = ((), (), s32[]{:S(2)}) async-start(), calls=%async_computation.17 | async-start | bytes 1253376 | tf_op jit(solution)/shard_map/reduce_scatter | solution.py:276
  514.6 220.6 %reduce-scatter.20.cloned.1.call-start = ((), (), s32[]{:S(2)}) async-start(), calls=%async_computation.22 | async-start | bytes 3342336 | tf_op jit(solution)/shard_map/reduce_scatter | solution.py:232
  522.1 282.2 %reduce-scatter.16.cloned.1.call-start = ((), (), s32[]{:S(2)}) async-start(), calls=%async_computation.20 | async-start | bytes 3342336 | tf_op jit(solution)/shard_map/reduce_scatter | solution.py:226
  530.6 342.7 %reduce-scatter.18.cloned.1.call-start = ((), (), s32[]{:S(2)}) async-start(), calls=%async_computation.21 | async-start | bytes 3342336 | tf_op jit(solution)/shard_map/reduce_scatter | solution.py:229
  531.5 4.9 collective-permute-start
  536.4 12.4 %collective-permute-start.1 = (bf16[256,768]{1,0:T(8,128)(2,1)S(1)}, bf16[256,768]{1,0:T(8,128)(2,1)S(1)}, u32[]{:S(2)}, u32[]{:S(2)}) collective-permute-start(bf16[256,768]{1,0:T(8,128)(2,1)S(1)} %pad_maximum_fusion.8), channel_id=1, source_target_pairs={{0,28},{2,30},{4,0},{6,2},{8,4},{10,6},{12,8},{14,10},{16,12},{18,... | collective-permute-start | bytes 1179656 | tf_op jit(solution)/shard_map/ppermute | solution.py:24
  549.8 20.8 %collective-permute-start.2 = (bf16[512,768]{1,0:T(8,128)(2,1)}, bf16[512,768]{1,0:T(8,128)(2,1)S(1)}, u32[]{:S(2)}, u32[]{:S(2)}) collective-permute-start(bf16[512,768]{1,0:T(8,128)(2,1)} %pad_maximum_fusion.7), channel_id=1, source_target_pairs={{0,24},{2,26},{4,28},{6,30},{8,0},{10,2},{12,4},{14,6},{16,8},{18,... | collective-permute-start | bytes 2359304 | tf_op jit(solution)/shard_map/ppermute | solution.py:24
  571.8 95.4 %collective-permute-start.3 = (bf16[1024,768]{1,0:T(8,128)(2,1)}, bf16[1024,768]{1,0:T(8,128)(2,1)S(1)}, u32[]{:S(2)}, u32[]{:S(2)}) collective-permute-start(bf16[1024,768]{1,0:T(8,128)(2,1)} %pad_maximum_fusion.1), channel_id=1, source_target_pairs={{0,16},{2,18},{4,20},{6,22},{8,24},{10,26},{12,28},{14,30},{16,0},... | collective-permute-start | bytes 4718600 | tf_op jit(solution)/shard_map/ppermute | solution.py:24
  582.8 335.0 %all-to-all-start.1 = ((bf16[16,64,768]{2,1,0:T(8,128)(2,1)}), bf16[16,64,768]{2,1,0:T(8,128)(2,1)}, u32[]{:S(2)}, u32[]{:S(2)}) async-start(bf16[16,64,768]{2,1,0:T(8,128)(2,1)} %bitcast.26), calls=%async_computation.1 | async-start | bytes 3145728 | tf_op jit(solution)/shard_map/all_to_all | solution.py:265
  588.7 342.1 %all-reduce.7.cloned.1.call-start = ((), (), s32[]{:S(2)}) async-start(), calls=%async_computation.23 | async-start | bytes 1769472 | tf_op jit(solution)/shard_map/psum | solution.py:294
  873.3 44.5 %copy-start.38 = (pred[16,64]{1,0:T(8,128)(4,1)S(1)}, pred[16,64]{1,0:T(8,128)(4,1)}, u32[]{:S(2)}) copy-start(pred[16,64]{1,0:T(8,128)(4,1)} %copy-done.37) | copy-start | bytes 3076
  921.2 20.9 %copy-start.1 = (bf16[1,512,768]{2,1,0:T(8,128)(2,1)S(1)}, bf16[1,512,768]{2,1,0:T(8,128)(2,1)}, u32[]{:S(2)}) copy-start(bf16[1,512,768]{2,1,0:T(8,128)(2,1)} %param.13) | copy-start | bytes 2359300
  (38 other events, 153.4 us)
Sparse Core Ops, SparseCore 0:
  10.3 51.5 all-gather.9
  64.1 39.0 all-gather.11
  105.6 37.1 all-gather.7
  144.9 37.1 all-gather.13
  184.2 44.3 all-gather.17
  230.8 43.8 all-gather.15
  276.9 43.8 all-gather.19
  353.4 56.4 reduce-scatter.13
  433.1 56.5 reduce-scatter.11
  496.5 58.0 reduce-scatter.7
  558.2 92.5 reduce-scatter.9
  654.5 80.6 reduce-scatter.19
  739.0 65.2 reduce-scatter.15
  808.0 65.2 reduce-scatter.17
  875.9 35.5 all-reduce.6
